TPU v7x, 256 devices: a whole 4x4x8 slice. The times are simulated.
256 devices in a mesh: rows: 128 (over x, z, y), cols: 2 (over core).
Axes of the slice: x: 4, y: 4, z: 8, core: 2. Of those that a mesh axis runs over, the one named last changes fastest.
Arguments:
- embeddings: bfloat16 [262144, 384], P('rows')
- test_matrix: bfloat16 [262144, 64], P('rows'), may hold values from -6 to 6
- pair_list: int32 [1024, 2], P(('rows', 'cols')), may hold values from -1 to 255, as said below
Outputs:
- orthonormal_basis: float32 [262144, 64], P(('rows', 'cols'))
- upper_factor: float32 [64, 64], replicated
Inputs may be any that keep to these rules, and one draw needn't show every extreme that they name: `pair_list`: device (r, c) holds 4 entries. Its live entries come first: pairs (i, j) with r * 2 <= i < (r + 1) * 2 and i <= j < min((r + 3) * 2, 256); each pair appears at most once over all devices; its other entries are -1 in both places. The device with c = 0 holds at least one live pair, the two devices of one r hold at most 4 together, and device (0, 0) holds exactly 4.
All inputs are finite; a program needn't handle non-finite values.
Results may differ from a plain program's by a relative error of at most 0.0053.
Values may be sent and summed in bfloat16 or wider, within the bound.
No kernel may reach another device: no remote copies, remote signals or barrier semaphores. Data moves between devices by JAX's collectives and lax.ppermute only.
A program may use at most 64 MiB of HBM per device.

v0:
```python
import jax
import jax.numpy as jnp
from jax import lax
from jax.sharding import PartitionSpec as P

BLK = 1024
SHARPNESS = 6.0
EPSILON = 1e-06


def shifted(value, axis, steps):
    count = lax.axis_size(axis)
    initial, last = (max(0, -steps), min(count, count - steps))
    return lax.ppermute(value, axis, [(source, source + steps) for source in range(initial, last)])


def unit_rows(embeddings):
    widened = embeddings.astype(jnp.float32)
    inverse = lax.rsqrt(jnp.sum(widened * widened, axis=1, keepdims=True) + EPSILON)
    return (widened * inverse).astype(jnp.bfloat16)


def affinity(left_rows, right_rows):
    scores = lax.dot_general(
        left_rows, right_rows, (((1,), (1,)), ((), ())), preferred_element_type=jnp.float32
    )
    return jnp.exp(SHARPNESS * (scores - 1.0)).astype(jnp.bfloat16)


def mirror_product(affinity_tile, vectors):
    return lax.dot_general(
        affinity_tile, vectors, (((0,), (0,)), ((), ())), preferred_element_type=jnp.float32
    )


def block_at(stacked, index):
    return lax.dynamic_index_in_dim(stacked, index, 0, keepdims=False)


def add_block(stacked, index, term):
    return lax.dynamic_update_index_in_dim(stacked, block_at(stacked, index) + term, index, 0)


def count_live(pair_rows):
    return jnp.sum((pair_rows[:, 0] >= 0).astype(jnp.int32))


def orthonormal(sketch_rows, rows_total):
    gram_matrix = lax.dot_general(
        sketch_rows,
        sketch_rows,
        (((0,), (0,)), ((), ())),
        precision=lax.Precision.HIGHEST,
        preferred_element_type=jnp.float32,
    )
    gram_matrix = lax.psum(gram_matrix, ("rows", "cols")) / rows_total
    lower_factor = jnp.linalg.cholesky(gram_matrix)
    solved = lax.linalg.triangular_solve(
        lower_factor, sketch_rows, left_side=False, lower=True, transpose_a=True
    )
    return (solved, lower_factor.T)


def affinity_pass(window_units, own_vectors, my_pairs, base_block):
    blocks_dev = own_vectors.shape[0]
    ahead_vectors = [shifted(own_vectors, "rows", -offset) for offset in (1, 2)]
    window_vectors = jnp.concatenate([own_vectors] + ahead_vectors, axis=0)
    initial = jnp.zeros(window_vectors.shape, jnp.float32)

    def pair_step(slot_index, accumulated):
        entry = my_pairs[slot_index]
        first_block = entry[0] - base_block
        second_block = entry[1] - base_block
        affinity_tile = affinity(
            block_at(window_units, first_block), block_at(window_units, second_block)
        )
        forward = jnp.dot(
            affinity_tile,
            block_at(window_vectors, second_block),
            preferred_element_type=jnp.float32,
        )
        accumulated = add_block(accumulated, first_block, forward)
        mirrored = first_block != second_block

        def add_mirror(current):
            return add_block(
                current,
                second_block,
                mirror_product(affinity_tile, block_at(window_vectors, first_block)),
            )

        return lax.cond(mirrored, add_mirror, lambda unchanged: unchanged, accumulated)

    accumulated = lax.fori_loop(0, count_live(my_pairs), pair_step, initial)
    own_blocks = accumulated[:blocks_dev]
    for offset in (1, 2):
        own_blocks = own_blocks + shifted(
            accumulated[offset * blocks_dev : (offset + 1) * blocks_dev], "rows", offset
        )
    flattened = own_blocks.reshape(-1, own_blocks.shape[2])
    return lax.psum_scatter(flattened, "cols", scatter_dimension=0, tiled=True)


def local(embeddings, test_matrix, pair_list):
    rows_dev = embeddings.shape[0]
    blocks_dev = rows_dev // BLK
    columns = test_matrix.shape[1]
    base_block = lax.axis_index("rows") * blocks_dev
    rows_total = rows_dev * lax.axis_size("rows")
    normed = unit_rows(embeddings).reshape(blocks_dev, BLK, embeddings.shape[1])
    ahead_units = [shifted(normed, "rows", -offset) for offset in (1, 2)]
    window_units = jnp.concatenate([normed] + ahead_units, axis=0)
    sketch_rows = affinity_pass(
        window_units, test_matrix.reshape(blocks_dev, BLK, columns), pair_list, base_block
    )
    panel_rows, _ = orthonormal(sketch_rows, rows_total)
    panel_whole = lax.all_gather(panel_rows.astype(jnp.bfloat16), "cols", axis=0, tiled=True)
    image_rows = affinity_pass(
        window_units, panel_whole.reshape(blocks_dev, BLK, columns), pair_list, base_block
    )
    return orthonormal(image_rows, rows_total)


def solution(mesh):
    in_specs = (P("rows", None), P("rows", None), P(("rows", "cols"), None))
    out_specs = (P(("rows", "cols"), None), P())
    return jax.shard_map(local, mesh=mesh, in_specs=in_specs, out_specs=out_specs, check_vma=False)
```

profile of v0, /device:TPU:1, one launch (start us, length us, event | category | flops | bytes accessed | tf_op | source)
XLA Modules:
  0.0 547.8 jit_solution(13680197383918252103)
XLA Ops:
  7.2 1.9 fusion.32
  15.7 85.9 %collective-permute-done.2 = bf16[2,1024,64]{2,1,0:T(8,128)(2,1)S(1)} collective-permute-done((bf16[2,1024,64]{2,1,0:T(8,128)(2,1)S(1)}, bf16[2,1024,64]{2,1,0:T(8,128)(2,1)S(1)}, u32[]{:S(2)}, u32[]{:S(2)}) %collective-permute-start.2) | collective-permute-done | bytes 262176 | tf_op jit(solution)/shard_map/ppermute | solution.py:14
  101.6 1.5 pad_maximum_fusion.1
  103.1 3.8 pad_maximum_fusion
  110.2 6.4 %collective-permute-start.4 = (f32[2,1024,64]{1,2,0:T(8,128)S(1)}, f32[2,1024,64]{1,2,0:T(8,128)S(1)}, u32[]{:S(2)}, u32[]{:S(2)}) collective-permute-start(f32[2,1024,64]{1,2,0:T(8,128)S(1)} %get-tuple-element.272), channel_id=1, source_target_pairs={{0,2},{2,4},{4,6},{6,8},{8,10},{10,12},{12,14},{14,16},{16,18},{18... | collective-permute-start | bytes 1572872 | tf_op jit(solution)/shard_map/ppermute | solution.py:14
  116.6 72.9 %collective-permute-start.5 = (f32[2,1024,64]{1,2,0:T(8,128)S(1)}, f32[2,1024,64]{1,2,0:T(8,128)S(1)}, u32[]{:S(2)}, u32[]{:S(2)}) collective-permute-start(f32[2,1024,64]{1,2,0:T(8,128)S(1)} %get-tuple-element.273), channel_id=1, source_target_pairs={{0,4},{2,6},{4,8},{6,10},{8,12},{10,14},{12,16},{14,18},{16,20},{1... | collective-permute-start | bytes 1572872 | tf_op jit(solution)/shard_map/ppermute | solution.py:14
  189.5 6.1 %collective-permute-done.5 = f32[2,1024,64]{1,2,0:T(8,128)S(1)} collective-permute-done((f32[2,1024,64]{1,2,0:T(8,128)S(1)}, f32[2,1024,64]{1,2,0:T(8,128)S(1)}, u32[]{:S(2)}, u32[]{:S(2)}) %collective-permute-start.5) | collective-permute-done | bytes 524320 | tf_op jit(solution)/shard_map/ppermute | solution.py:14
  197.7 36.3 %reduce-scatter.3.cloned.1.call-done = f32[1024,64]{0,1:T(8,128)} async-done(((f32[2048,64]{0,1:T(8,128)}), f32[1024,64]{0,1:T(8,128)}) %reduce-scatter.3.cloned.1.call-update) | async-done | bytes 262160 | tf_op jit(solution)/shard_map/reduce_scatter | solution.py:101
  234.0 1.4 fusion.49
  235.5 77.5 %psum.14 = f32[64,64]{0,1:T(8,128)S(1)} all-reduce(f32[64,64]{0,1:T(8,128)S(1)} %fusion.49), channel_id=1, replica_groups=mesh['rows'=128,'cols'=2] {'rows','cols'}, use_global_device_ids=true, to_apply=%region_7.8 | all-reduce | flops 4096 | bytes 32768 | tf_op jit(solution)/shard_map/psum | solution.py:56
  313.1 5.8 %cholesky.44 = f32[64,64]{1,0:T(8,128)S(1)} custom-call(f32[64,64]{1,0:T(8,128)S(1)} %fusion.39), custom_call_target="Cholesky" | custom-call | tf_op jit(solution)/shard_map/jit(cholesky)/cholesky | solution.py:57
  320.3 4.9 custom-call.6
  326.6 2.5 all_gather.3
  332.0 22.3 %collective-permute-done.6 = bf16[2,1024,64]{2,1,0:T(8,128)(2,1)S(1)} collective-permute-done((bf16[2,1024,64]{2,1,0:T(8,128)(2,1)S(1)}, bf16[2,1024,64]{2,1,0:T(8,128)(2,1)S(1)}, u32[]{:S(2)}, u32[]{:S(2)}) %collective-permute-start.6) | collective-permute-done | bytes 262176 | tf_op jit(solution)/shard_map/ppermute | solution.py:14
  354.2 1.5 pad_maximum_fusion.2
  359.1 3.7 collective-permute-start.8
  362.7 45.1 %collective-permute-start.9 = (f32[2,1024,64]{1,2,0:T(8,128)S(1)}, f32[2,1024,64]{1,2,0:T(8,128)S(1)}, u32[]{:S(2)}, u32[]{:S(2)}) collective-permute-start(f32[2,1024,64]{1,2,0:T(8,128)S(1)} %get-tuple-element.271), channel_id=1, source_target_pairs={{0,4},{2,6},{4,8},{6,10},{8,12},{10,14},{12,16},{14,18},{16,20},{1... | collective-permute-start | bytes 1572872 | tf_op jit(solution)/shard_map/ppermute | solution.py:14
  407.8 11.5 %collective-permute-done.9 = f32[2,1024,64]{1,2,0:T(8,128)S(1)} collective-permute-done((f32[2,1024,64]{1,2,0:T(8,128)S(1)}, f32[2,1024,64]{1,2,0:T(8,128)S(1)}, u32[]{:S(2)}, u32[]{:S(2)}) %collective-permute-start.9) | collective-permute-done | bytes 524320 | tf_op jit(solution)/shard_map/ppermute | solution.py:14
  421.3 25.8 %reduce-scatter.5.cloned.1.call-done = f32[1024,64]{0,1:T(8,128)} async-done(((f32[2048,64]{0,1:T(8,128)}), f32[1024,64]{0,1:T(8,128)}) %reduce-scatter.5.cloned.1.call-update) | async-done | bytes 262160 | tf_op jit(solution)/shard_map/reduce_scatter | solution.py:101
  447.1 1.4 fusion.50
  448.4 77.5 %psum.15 = f32[64,64]{0,1:T(8,128)S(1)} all-reduce(f32[64,64]{0,1:T(8,128)S(1)} %fusion.50), channel_id=1, replica_groups=mesh['rows'=128,'cols'=2] {'rows','cols'}, use_global_device_ids=true, to_apply=%region_15.18 | all-reduce | flops 4096 | bytes 32768 | tf_op jit(solution)/shard_map/psum | solution.py:56
  526.1 5.8 %cholesky.55 = f32[64,64]{1,0:T(8,128)S(1)} custom-call(f32[64,64]{1,0:T(8,128)S(1)} %fusion.37), custom_call_target="Cholesky" | custom-call | tf_op jit(solution)/shard_map/jit(cholesky)/cholesky | solution.py:57
  533.3 4.9 custom-call.7
  538.9 2.1 convolution_bitcast_fusion.2
  (51 shorter events, 24.9 us)
Async XLA Ops:
  7.2 2.0 copy-start
  7.2 226.9 %reduce-scatter.3.cloned.1.call-start = ((), (), s32[]{:S(2)}) async-start(), calls=%async_computation.2 | async-start | bytes 786432 | tf_op jit(solution)/shard_map/reduce_scatter | solution.py:101
  9.1 3.0 copy-start.1
  9.2 5.9 %copy-start.2 = (s32[4,2]{0,1:T(2,128)S(1)}, s32[4,2]{0,1:T(2,128)}, u32[]{:S(2)}) copy-start(s32[4,2]{0,1:T(2,128)} %param.16) | copy-start | bytes 100
  9.5 93.6 %collective-permute-start = (bf16[2,1024,384]{2,1,0:T(8,128)(2,1)S(1)}, bf16[2,1024,384]{2,1,0:T(8,128)(2,1)}, u32[]{:S(2)}, u32[]{:S(2)}) collective-permute-start(bf16[2,1024,384]{2,1,0:T(8,128)(2,1)S(1)} %bitcast.145), channel_id=1, source_target_pairs={{2,0},{4,2},{6,4},{8,6},{10,8},{12,10},{14,12},{16,14},{18,16},{20... | collective-permute-start | bytes 4718600 | tf_op jit(solution)/shard_map/ppermute | solution.py:14
  10.8 92.3 %collective-permute-start.1 = (bf16[2,1024,384]{2,1,0:T(8,128)(2,1)S(1)}, bf16[2,1024,384]{2,1,0:T(8,128)(2,1)}, u32[]{:S(2)}, u32[]{:S(2)}) collective-permute-start(bf16[2,1024,384]{2,1,0:T(8,128)(2,1)S(1)} %bitcast.146), channel_id=1, source_target_pairs={{4,0},{6,2},{8,4},{10,6},{12,8},{14,10},{16,12},{18,14},{20,16},{2... | collective-permute-start | bytes 4718600 | tf_op jit(solution)/shard_map/ppermute | solution.py:14
  12.4 89.2 %collective-permute-start.2 = (bf16[2,1024,64]{2,1,0:T(8,128)(2,1)S(1)}, bf16[2,1024,64]{2,1,0:T(8,128)(2,1)S(1)}, u32[]{:S(2)}, u32[]{:S(2)}) collective-permute-start(bf16[2,1024,64]{2,1,0:T(8,128)(2,1)S(1)} %bitcast.150), channel_id=1, source_target_pairs={{2,0},{4,2},{6,4},{8,6},{10,8},{12,10},{14,12},{16,14},{18,16},{20... | collective-permute-start | bytes 786440 | tf_op jit(solution)/shard_map/ppermute | solution.py:14
  13.7 87.9 %collective-permute-start.3 = (bf16[2,1024,64]{2,1,0:T(8,128)(2,1)S(1)}, bf16[2,1024,64]{2,1,0:T(8,128)(2,1)S(1)}, u32[]{:S(2)}, u32[]{:S(2)}) collective-permute-start(bf16[2,1024,64]{2,1,0:T(8,128)(2,1)S(1)} %bitcast.151), channel_id=1, source_target_pairs={{4,0},{6,2},{8,4},{10,6},{12,8},{14,10},{16,12},{18,14},{20,16},{2... | collective-permute-start | bytes 786440 | tf_op jit(solution)/shard_map/ppermute | solution.py:14
  110.2 79.3 %collective-permute-start.4 = (f32[2,1024,64]{1,2,0:T(8,128)S(1)}, f32[2,1024,64]{1,2,0:T(8,128)S(1)}, u32[]{:S(2)}, u32[]{:S(2)}) collective-permute-start(f32[2,1024,64]{1,2,0:T(8,128)S(1)} %get-tuple-element.272), channel_id=1, source_target_pairs={{0,2},{2,4},{4,6},{6,8},{8,10},{10,12},{12,14},{14,16},{16,18},{18... | collective-permute-start | bytes 1572872 | tf_op jit(solution)/shard_map/ppermute | solution.py:14
  116.6 79.0 %collective-permute-start.5 = (f32[2,1024,64]{1,2,0:T(8,128)S(1)}, f32[2,1024,64]{1,2,0:T(8,128)S(1)}, u32[]{:S(2)}, u32[]{:S(2)}) collective-permute-start(f32[2,1024,64]{1,2,0:T(8,128)S(1)} %get-tuple-element.273), channel_id=1, source_target_pairs={{0,4},{2,6},{4,8},{6,10},{8,12},{10,14},{12,16},{14,18},{16,20},{1... | collective-permute-start | bytes 1572872 | tf_op jit(solution)/shard_map/ppermute | solution.py:14
  197.7 249.4 %reduce-scatter.5.cloned.1.call-start = ((), (), s32[]{:S(2)}) async-start(), calls=%async_computation.3 | async-start | bytes 786432 | tf_op jit(solution)/shard_map/reduce_scatter | solution.py:101
  329.4 24.9 %collective-permute-start.6 = (bf16[2,1024,64]{2,1,0:T(8,128)(2,1)S(1)}, bf16[2,1024,64]{2,1,0:T(8,128)(2,1)S(1)}, u32[]{:S(2)}, u32[]{:S(2)}) collective-permute-start(bf16[2,1024,64]{2,1,0:T(8,128)(2,1)S(1)} %bitcast.153), channel_id=1, source_target_pairs={{2,0},{4,2},{6,4},{8,6},{10,8},{12,10},{14,12},{16,14},{18,16},{20... | collective-permute-start | bytes 786440 | tf_op jit(solution)/shard_map/ppermute | solution.py:14
  330.7 23.6 %collective-permute-start.7 = (bf16[2,1024,64]{2,1,0:T(8,128)(2,1)S(1)}, bf16[2,1024,64]{2,1,0:T(8,128)(2,1)S(1)}, u32[]{:S(2)}, u32[]{:S(2)}) collective-permute-start(bf16[2,1024,64]{2,1,0:T(8,128)(2,1)S(1)} %bitcast.154), channel_id=1, source_target_pairs={{4,0},{6,2},{8,4},{10,6},{12,8},{14,10},{16,12},{18,14},{20,16},{2... | collective-permute-start | bytes 786440 | tf_op jit(solution)/shard_map/ppermute | solution.py:14
  359.1 48.8 %collective-permute-start.8 = (f32[2,1024,64]{1,2,0:T(8,128)S(1)}, f32[2,1024,64]{1,2,0:T(8,128)S(1)}, u32[]{:S(2)}, u32[]{:S(2)}) collective-permute-start(f32[2,1024,64]{1,2,0:T(8,128)S(1)} %get-tuple-element.270), channel_id=1, source_target_pairs={{0,2},{2,4},{4,6},{6,8},{8,10},{10,12},{12,14},{14,16},{16,18},{18... | collective-permute-start | bytes 1572872 | tf_op jit(solution)/shard_map/ppermute | solution.py:14
  362.7 56.6 %collective-permute-start.9 = (f32[2,1024,64]{1,2,0:T(8,128)S(1)}, f32[2,1024,64]{1,2,0:T(8,128)S(1)}, u32[]{:S(2)}, u32[]{:S(2)}) collective-permute-start(f32[2,1024,64]{1,2,0:T(8,128)S(1)} %get-tuple-element.271), channel_id=1, source_target_pairs={{0,4},{2,6},{4,8},{6,10},{8,12},{10,14},{12,16},{14,18},{16,20},{1... | collective-permute-start | bytes 1572872 | tf_op jit(solution)/shard_map/ppermute | solution.py:14
Sparse Core Ops, SparseCore 0:
  197.8 36.2 reduce-scatter.2
  421.4 25.5 reduce-scatter.4
where the time goes:
time: 550 us; the launch traced here: 548 us
  waiting for transfers between devices  188 us (34%)
  blocking collectives  158 us (29%)
  starting transfers between devices  136 us (25%)
  other arithmetic  36.2 us (7%)
  between operations  14.3 us (3%)
  local copies, waits for them, and re-layouts  8.38 us (2%)
  matrix products  6.27 us (1%)
    psum x2, blocking collectives, orthonormal(): gram_matrix = lax.psum(gram_matrix, ('rows', 'cols')) / rows_total  155 us
    ppermute x10, starting transfers between devices, shifted(): lax.ppermute(value, axis, [(source, source + steps) for source in range(i...  136 us
    ppermute x10, waiting for transfers between devices, shifted(): lax.ppermute(value, axis, [(source, source + steps) for source in range(i...  126 us
    reduce_scatter x2, waiting for transfers between devices, affinity_pass(): return lax.psum_scatter(flattened, 'cols', scatter_dimension=0, tiled=True)  62.1 us
    another operation x6, other arithmetic, orthonormal(): lower_factor = jnp.linalg.cholesky(gram_matrix)  13 us
  transfers between devices with their start and end apart: 12, of which 6 were waited for; matrix products, arithmetic and copies ran while one was open for 0% of the time, Pallas kernels for 0%

commit v1 on v0

--- a/solution.py
+++ b/solution.py
@@ -53,7 +53,7 @@
         precision=lax.Precision.HIGHEST,
         preferred_element_type=jnp.float32,
     )
-    gram_matrix = lax.psum(gram_matrix, ("rows", "cols")) / rows_total
+    gram_matrix = lax.psum(lax.psum(gram_matrix, "cols"), "rows") / rows_total
     lower_factor = jnp.linalg.cholesky(gram_matrix)
     solved = lax.linalg.triangular_solve(
         lower_factor, sketch_rows, left_side=False, lower=True, transpose_a=True

time: 550 us -> 1760 us (3.20)
  the two profiles are of different devices: /device:TPU:1 before, /device:TPU:0 now
where the time goes in v1:
time: 1760 us; the launch traced here: 1750 us
  blocking collectives  1390 us (79%)
  waiting for transfers between devices  178 us (10%)
  matrix products  60.4 us (3%)
  other arithmetic  36.2 us (2%)
  starting transfers between devices  35 us (2%)
  local copies, waits for them, and re-layouts  26.9 us (2%)
    psum x4, blocking collectives, orthonormal(): gram_matrix = lax.psum(lax.psum(gram_matrix, 'cols'), 'rows') / rows_total  1390 us
    ppermute x10, waiting for transfers between devices, shifted(): lax.ppermute(value, axis, [(source, source + steps) for source in range(i...  127 us
    reduce_scatter x2, waiting for transfers between devices, affinity_pass(): return lax.psum_scatter(flattened, 'cols', scatter_dimension=0, tiled=True)  50.7 us
  transfers between devices with their start and end apart: 12, of which 7 were waited for; matrix products, arithmetic and copies ran while one was open for 0% of the time, Pallas kernels for 0%

profile of v1, /device:TPU:0, one launch (start us, length us, event | category | flops | bytes accessed | tf_op | source)
XLA Modules:
  0.0 1754.7 jit_solution(13738528905612419530)
XLA Ops:
  15.7 86.2 %collective-permute-done.2 = bf16[2,1024,64]{2,1,0:T(8,128)(2,1)S(1)} collective-permute-done((bf16[2,1024,64]{2,1,0:T(8,128)(2,1)S(1)}, bf16[2,1024,64]{2,1,0:T(8,128)(2,1)S(1)}, u32[]{:S(2)}, u32[]{:S(2)}) %collective-permute-start.2) | collective-permute-done | bytes 262176 | tf_op jit(solution)/shard_map/ppermute | solution.py:14
  103.4 3.8 pad_maximum_fusion
  108.5 44.5 %while.24 = (s32[]{:T(128)}, f32[6,1024,64]{1,2,0:T(8,128)}, s32[]{:T(128)}, s32[4,2]{0,1:T(2,128)S(1)}, s32[]{:T(128)}, /*index=5*/bf16[6,1024,384]{2,1,0:T(8,1...) while((s32[]{:T(128)}, f32[6,1024,64]{1,2,0:T(8,128)}, ...), condition=%wide.region_5.6_spmd, body=%wide.region_2.5_spmd.sunk | while | flops 1077018624 | bytes 10486193 | solution.py:94
  125.8 3.1 conditional.4
  137.5 3.2 conditional.4
  155.7 23.2 %collective-permute-start.5 = (f32[2,1024,64]{1,2,0:T(8,128)S(1)}, f32[2,1024,64]{1,2,0:T(8,128)S(1)}, u32[]{:S(2)}, u32[]{:S(2)}) collective-permute-start(f32[2,1024,64]{1,2,0:T(8,128)S(1)} %get-tuple-element.273), channel_id=1, source_target_pairs={{0,4},{2,6},{4,8},{6,10},{8,12},{10,14},{12,16},{14,18},{16,20},{1... | collective-permute-start | bytes 1572872 | tf_op jit(solution)/shard_map/ppermute | solution.py:14
  178.9 6.7 collective-permute-done.5
  187.6 42.7 %reduce-scatter.3.cloned.1.call-done = f32[1024,64]{0,1:T(8,128)} async-done(((f32[2048,64]{0,1:T(8,128)}), f32[1024,64]{0,1:T(8,128)}) %reduce-scatter.3.cloned.1.call-update) | async-done | bytes 262160 | tf_op jit(solution)/shard_map/reduce_scatter | solution.py:101
  231.8 3.9 psum.28
  235.7 688.8 %psum.29 = f32[64,64]{0,1:T(8,128)S(1)} all-reduce(f32[64,64]{0,1:T(8,128)S(1)} %psum.28), channel_id=1, replica_groups=mesh['rows'=128,'cols'=2] {'rows'}, use_global_device_ids=true, to_apply=%region_8.9 | all-reduce | flops 4096 | bytes 32768 | tf_op jit(solution)/shard_map/psum | solution.py:56
  924.6 5.8 cholesky.44
  931.8 4.9 custom-call.6
  942.9 23.3 %collective-permute-done.6 = bf16[2,1024,64]{2,1,0:T(8,128)(2,1)S(1)} collective-permute-done((bf16[2,1024,64]{2,1,0:T(8,128)(2,1)S(1)}, bf16[2,1024,64]{2,1,0:T(8,128)(2,1)S(1)}, u32[]{:S(2)}, u32[]{:S(2)}) %collective-permute-start.6) | collective-permute-done | bytes 262176 | tf_op jit(solution)/shard_map/ppermute | solution.py:14
  969.1 44.5 %while.25 = (s32[]{:T(128)}, f32[6,1024,64]{1,2,0:T(8,128)}, s32[]{:T(128)}, s32[4,2]{0,1:T(2,128)S(1)}, s32[]{:T(128)}, /*index=5*/bf16[6,1024,384]{2,1,0:T(8,1...) while((s32[]{:T(128)}, f32[6,1024,64]{1,2,0:T(8,128)}, ...), condition=%wide.region_14.17_spmd, body=%wide.region_11.0_spmd.sunk | while | flops 1077018624 | bytes 10486193 | solution.py:94
  986.3 3.1 conditional.5
  998.0 3.2 conditional.5
  1009.8 3.1 conditional.5
  1017.6 5.3 collective-permute-done.8
  1022.9 5.6 collective-permute-done.9
  1030.5 8.0 reduce-scatter.5.cloned.1.call-done
  1040.0 3.9 psum.30
  1043.8 689.0 %psum.31 = f32[64,64]{0,1:T(8,128)S(1)} all-reduce(f32[64,64]{0,1:T(8,128)S(1)} %psum.30), channel_id=1, replica_groups=mesh['rows'=128,'cols'=2] {'rows'}, use_global_device_ids=true, to_apply=%region_17.20 | all-reduce | flops 4096 | bytes 32768 | tf_op jit(solution)/shard_map/psum | solution.py:56
  1733.0 5.8 cholesky.55
  1740.2 4.9 custom-call.7
  (113 shorter events, 115.1 us)
Async XLA Ops:
  7.2 2.0 copy-start
  7.2 223.2 %reduce-scatter.3.cloned.1.call-start = ((), (), s32[]{:S(2)}) async-start(), calls=%async_computation.2 | async-start | bytes 786432 | tf_op jit(solution)/shard_map/reduce_scatter | solution.py:101
  9.1 3.0 copy-start.1
  9.2 5.9 copy-start.2
  9.5 93.8 %collective-permute-start = (bf16[2,1024,384]{2,1,0:T(8,128)(2,1)S(1)}, bf16[2,1024,384]{2,1,0:T(8,128)(2,1)}, u32[]{:S(2)}, u32[]{:S(2)}) collective-permute-start(bf16[2,1024,384]{2,1,0:T(8,128)(2,1)S(1)} %bitcast.145), channel_id=1, source_target_pairs={{2,0},{4,2},{6,4},{8,6},{10,8},{12,10},{14,12},{16,14},{18,16},{20... | collective-permute-start | bytes 4718600 | tf_op jit(solution)/shard_map/ppermute | solution.py:14
  10.8 92.5 %collective-permute-start.1 = (bf16[2,1024,384]{2,1,0:T(8,128)(2,1)S(1)}, bf16[2,1024,384]{2,1,0:T(8,128)(2,1)}, u32[]{:S(2)}, u32[]{:S(2)}) collective-permute-start(bf16[2,1024,384]{2,1,0:T(8,128)(2,1)S(1)} %bitcast.146), channel_id=1, source_target_pairs={{4,0},{6,2},{8,4},{10,6},{12,8},{14,10},{16,12},{18,14},{20,16},{2... | collective-permute-start | bytes 4718600 | tf_op jit(solution)/shard_map/ppermute | solution.py:14
  12.4 89.4 %collective-permute-start.2 = (bf16[2,1024,64]{2,1,0:T(8,128)(2,1)S(1)}, bf16[2,1024,64]{2,1,0:T(8,128)(2,1)S(1)}, u32[]{:S(2)}, u32[]{:S(2)}) collective-permute-start(bf16[2,1024,64]{2,1,0:T(8,128)(2,1)S(1)} %bitcast.150), channel_id=1, source_target_pairs={{2,0},{4,2},{6,4},{8,6},{10,8},{12,10},{14,12},{16,14},{18,16},{20... | collective-permute-start | bytes 786440 | tf_op jit(solution)/shard_map/ppermute | solution.py:14
  13.7 88.1 %collective-permute-start.3 = (bf16[2,1024,64]{2,1,0:T(8,128)(2,1)S(1)}, bf16[2,1024,64]{2,1,0:T(8,128)(2,1)S(1)}, u32[]{:S(2)}, u32[]{:S(2)}) collective-permute-start(bf16[2,1024,64]{2,1,0:T(8,128)(2,1)S(1)} %bitcast.151), channel_id=1, source_target_pairs={{4,0},{6,2},{8,4},{10,6},{12,8},{14,10},{16,12},{18,14},{20,16},{2... | collective-permute-start | bytes 786440 | tf_op jit(solution)/shard_map/ppermute | solution.py:14
  154.4 24.5 %collective-permute-start.4 = (f32[2,1024,64]{1,2,0:T(8,128)S(1)}, f32[2,1024,64]{1,2,0:T(8,128)S(1)}, u32[]{:S(2)}, u32[]{:S(2)}) collective-permute-start(f32[2,1024,64]{1,2,0:T(8,128)S(1)} %get-tuple-element.272), channel_id=1, source_target_pairs={{0,2},{2,4},{4,6},{6,8},{8,10},{10,12},{12,14},{14,16},{16,18},{18... | collective-permute-start | bytes 1572872 | tf_op jit(solution)/shard_map/ppermute | solution.py:14
  155.7 29.9 %collective-permute-start.5 = (f32[2,1024,64]{1,2,0:T(8,128)S(1)}, f32[2,1024,64]{1,2,0:T(8,128)S(1)}, u32[]{:S(2)}, u32[]{:S(2)}) collective-permute-start(f32[2,1024,64]{1,2,0:T(8,128)S(1)} %get-tuple-element.273), channel_id=1, source_target_pairs={{0,4},{2,6},{4,8},{6,10},{8,12},{10,14},{12,16},{14,18},{16,20},{1... | collective-permute-start | bytes 1572872 | tf_op jit(solution)/shard_map/ppermute | solution.py:14
  187.6 851.0 %reduce-scatter.5.cloned.1.call-start = ((), (), s32[]{:S(2)}) async-start(), calls=%async_computation.3 | async-start | bytes 786432 | tf_op jit(solution)/shard_map/reduce_scatter | solution.py:101
  940.3 25.9 %collective-permute-start.6 = (bf16[2,1024,64]{2,1,0:T(8,128)(2,1)S(1)}, bf16[2,1024,64]{2,1,0:T(8,128)(2,1)S(1)}, u32[]{:S(2)}, u32[]{:S(2)}) collective-permute-start(bf16[2,1024,64]{2,1,0:T(8,128)(2,1)S(1)} %bitcast.153), channel_id=1, source_target_pairs={{2,0},{4,2},{6,4},{8,6},{10,8},{12,10},{14,12},{16,14},{18,16},{20... | collective-permute-start | bytes 786440 | tf_op jit(solution)/shard_map/ppermute | solution.py:14
  941.6 24.6 %collective-permute-start.7 = (bf16[2,1024,64]{2,1,0:T(8,128)(2,1)S(1)}, bf16[2,1024,64]{2,1,0:T(8,128)(2,1)S(1)}, u32[]{:S(2)}, u32[]{:S(2)}) collective-permute-start(bf16[2,1024,64]{2,1,0:T(8,128)(2,1)S(1)} %bitcast.154), channel_id=1, source_target_pairs={{4,0},{6,2},{8,4},{10,6},{12,8},{14,10},{16,12},{18,14},{20,16},{2... | collective-permute-start | bytes 786440 | tf_op jit(solution)/shard_map/ppermute | solution.py:14
  1014.9 8.0 collective-permute-start.8
  1016.2 12.3 collective-permute-start.9
Sparse Core Ops, SparseCore 0:
  187.7 42.5 reduce-scatter.2
  1030.6 7.8 reduce-scatter.4
